TPU v7x, 32 devices: a whole 2x2x4 slice. The times are simulated.
32 devices in a mesh: group: 2 (over x), col: 16 (over z, y, core).
Axes of the slice: x: 2, y: 2, z: 4, core: 2. Of those that a mesh axis runs over, the one named last changes fastest.
Arguments:
- homolog_embedding: bfloat16 [192, 64, 256], P('group', 'col'), parts along dimension 0, may hold values from -6 to 6
- left_factor_matrix: bfloat16 [256, 32], replicated, may hold values from -0.375 to 0.375
- right_factor_matrix: bfloat16 [256, 32], replicated, may hold values from -0.375 to 0.375
- decoder: bfloat16 [1024, 128], replicated, may hold values from -2 to 2
- pair_output_bias: float32 [128], replicated, may hold values from -3 to 3
- pair_output_gradient: bfloat16 [128, 64, 128], P('group', 'col'), parts along dimension 0, may hold values from -6 to 6
Outputs:
- first_operand_gradient: float32 [192, 64, 32], P('group', 'col'), parts along dimension 0
- second_operand_gradient: float32 [192, 64, 32], P('group', 'col'), parts along dimension 0
- alignment_gradient: bfloat16 [192, 64, 256], P('group', 'col'), parts along dimension 0
There are 2 independent parts, one for each index of `group`. A program takes and returns all parts, laid end to end along the dimension named above; an argument that names none is the same for every part. Nothing has to cross between parts.
All inputs are finite; a program needn't handle non-finite values.
Results may differ from a plain program's by a relative error of at most 0.0083.
Values may be sent and summed in bfloat16 or wider, within the bound.
A program may use at most 64 MiB of HBM per device.

v0:
```python
import jax
import jax.numpy as jnp
from jax import lax
from jax.sharding import PartitionSpec as P


def per_device(
    homolog_embedding,
    left_factor_matrix,
    right_factor_matrix,
    decoder,
    pair_output_bias,
    pair_output_gradient,
):
    alignment_row_count, local_residue_start, alignment_channel_width = homolog_embedding.shape
    operand_channel_width = left_factor_matrix.shape[1]
    channels = decoder.shape[1]
    residue_total_count = local_residue_start * lax.axis_size("col")
    reciprocal_rows = 1.0 / alignment_row_count
    block_res = local_residue_start * max(1, 96 // local_residue_start)
    alignment_flattened_rows = homolog_embedding.reshape(
        alignment_row_count * local_residue_start, alignment_channel_width
    )
    first_operand_rows = (
        jnp.dot(alignment_flattened_rows, left_factor_matrix, preferred_element_type=jnp.float32)
        .astype(jnp.bfloat16)
        .reshape(alignment_row_count, local_residue_start * operand_channel_width)
    )
    second_operand_rows = (
        jnp.dot(alignment_flattened_rows, right_factor_matrix, preferred_element_type=jnp.float32)
        .astype(jnp.bfloat16)
        .reshape(alignment_row_count, local_residue_start * operand_channel_width)
    )
    second_operand_local = second_operand_rows.reshape(
        alignment_row_count, local_residue_start, operand_channel_width
    )

    def outer_slopes(slope_rows, rows_by_length, col_span):
        backward = (
            jnp.dot(slope_rows, decoder.T, preferred_element_type=jnp.float32) * reciprocal_rows
        )
        return backward.astype(jnp.bfloat16).reshape(
            rows_by_length, col_span, operand_channel_width, operand_channel_width
        )

    offset_col = jnp.int32(0)
    second_operand_gradient = jnp.zeros(
        (alignment_row_count, local_residue_start, operand_channel_width), jnp.float32
    )
    stored = jnp.zeros((residue_total_count, local_residue_start * channels), jnp.bfloat16)
    left_segment = lax.all_gather(first_operand_rows, "col", axis=1, tiled=True)
    right_segment = lax.all_gather(second_operand_rows, "col", axis=1, tiled=True)
    right_whole = right_segment
    piece_res = left_segment.shape[1] // operand_channel_width
    first_res = offset_col // operand_channel_width
    collected = []
    for split_offset in range(0, piece_res, block_res):
        split_rows_by_length = min(block_res, piece_res - split_offset)
        split_left_block = left_segment[
            :,
            split_offset
            * operand_channel_width : (split_offset + split_rows_by_length)
            * operand_channel_width,
        ].reshape(alignment_row_count, split_rows_by_length, operand_channel_width)
        collected.append((split_rows_by_length, split_left_block, first_res + split_offset))
    for rows_by_length, left_block, first_row in collected:
        products = (
            jnp.einsum(
                "sic,sjd->ijcd",
                left_block,
                second_operand_local,
                preferred_element_type=jnp.float32,
            )
            * reciprocal_rows
        )
        products = products.astype(jnp.bfloat16).reshape(
            rows_by_length * local_residue_start, operand_channel_width * operand_channel_width
        )
        linear = jnp.dot(products, decoder, preferred_element_type=jnp.float32) + pair_output_bias
        upstream = lax.dynamic_slice_in_dim(pair_output_gradient, first_row, rows_by_length, 0)
        upstream = upstream.reshape(rows_by_length * local_residue_start, channels).astype(
            jnp.float32
        )
        accumulate_slope_rows = (upstream * 2.0 * jnp.maximum(linear, 0.0)).astype(jnp.bfloat16)
        stored = lax.dynamic_update_slice_in_dim(
            stored,
            accumulate_slope_rows.reshape(rows_by_length, local_residue_start * channels),
            first_row,
            0,
        )
        accumulate_slopes = outer_slopes(accumulate_slope_rows, rows_by_length, local_residue_start)
        second_operand_gradient = second_operand_gradient + jnp.einsum(
            "ijcd,sic->sjd", accumulate_slopes, left_block, preferred_element_type=jnp.float32
        )
    second_operand_gradient, stored, right_whole = (second_operand_gradient, stored, right_whole)
    received = lax.all_to_all(stored, "col", split_axis=0, concat_axis=1, tiled=True)
    right_all = right_whole.reshape(alignment_row_count, residue_total_count, operand_channel_width)
    col_span = local_residue_start * max(
        max(1, 96 // local_residue_start), lax.axis_size("col") // 8
    )
    first_operand_gradient = jnp.zeros(
        (alignment_row_count, local_residue_start, operand_channel_width), jnp.float32
    )
    for offset in range(0, residue_total_count, col_span):
        width_cols = min(col_span, residue_total_count - offset)
        slope_rows = received[:, offset * channels : (offset + width_cols) * channels].reshape(
            local_residue_start * width_cols, channels
        )
        slopes = outer_slopes(slope_rows, local_residue_start, width_cols)
        first_operand_gradient = first_operand_gradient + jnp.einsum(
            "ijcd,sjd->sic",
            slopes,
            right_all[:, offset : offset + width_cols],
            preferred_element_type=jnp.float32,
        )
    first_operand_gradient_step = first_operand_gradient.astype(jnp.bfloat16).reshape(
        alignment_row_count * local_residue_start, operand_channel_width
    )
    second_operand_gradient_step = second_operand_gradient.astype(jnp.bfloat16).reshape(
        alignment_row_count * local_residue_start, operand_channel_width
    )
    alignment_gradient = jnp.dot(
        first_operand_gradient_step, left_factor_matrix.T, preferred_element_type=jnp.float32
    ) + jnp.dot(
        second_operand_gradient_step, right_factor_matrix.T, preferred_element_type=jnp.float32
    )
    alignment_gradient = alignment_gradient.astype(jnp.bfloat16).reshape(
        alignment_row_count, local_residue_start, alignment_channel_width
    )
    return (first_operand_gradient, second_operand_gradient, alignment_gradient)


def solution(mesh):
    placed = (P("group", "col", None), P(), P(), P(), P(), P("group", "col", None))
    return jax.shard_map(
        per_device,
        mesh=mesh,
        in_specs=placed,
        out_specs=(P("group", "col", None), P("group", "col", None), P("group", "col", None)),
        check_vma=False,
    )
```

profile of v0, /device:TPU:0, one launch (start us, length us, event | category | flops | bytes accessed | tf_op | source)
XLA Modules:
  0.0 74.2 jit_solution(9161705522396213601)
XLA Ops:
  0.6 0.0 copy-start
  0.7 1.0 %reshape.53 = bf16[384,256]{1,0:T(8,128)(2,1)S(1)} reshape(bf16[96,4,256]{2,1,0:T(4,128)(2,1)} %param.6) | data formatting | bytes 393216 | tf_op jit(solution)/shard_map/reshape | solution.py:21
  1.7 0.9 %convolution_convert_fusion = bf16[384,32]{0,1:T(8,128)(2,1)S(1)} fusion(bf16[384,256]{1,0:T(8,128)(2,1)S(1)} %reshape.53, bf16[256,32]{0,1:T(8,128)(2,1)} %param.7), kind=kOutput, calls=%fused_computation.14 | convolution fusion | flops 6303744 | bytes 237568 | tf_op jit(solution)/shard_map/dot_general | solution.py:25
  2.6 0.1 copy.31
  2.7 0.1 reshape.56
  2.8 24.2 %all_gather.7 = bf16[96,2048]{1,0:T(8,128)(2,1)S(1)} all-gather(bf16[96,128]{1,0:T(8,128)(2,1)S(1)} %reshape.56), channel_id=1, replica_groups=mesh['group'=2,'col'=16] {'col'}, dimensions={1}, use_global_device_ids=true | all-gather | bytes 417792 | tf_op jit(solution)/shard_map/all_gather | solution.py:51
  27.0 0.3 copy.32
  27.3 0.2 convolution_convert_fusion.1
  27.5 0.1 copy.28
  27.6 1.6 %fusion = bf16[64,4,32,32]{0,3,2,1:T(8,128)(2,1)} fusion(bf16[96,64,32]{0,2,1:T(8,128)(2,1)S(1)} %bitcast.48, bf16[96,4,32,1]{2,1,0,3:T(4,128)(2,1)S(1)} %bitcast.51), kind=kOutput, calls=%fused_computation.1 | convolution fusion | flops 50855936 | bytes 942080 | tf_op jit(solution)/shard_map/sic,sjd->ijcd/dot_general | solution.py:68
  29.3 4.2 %copy.35 = bf16[64,4,32,32]{3,2,1,0:T(8,128)(2,1)S(1)} copy(bf16[64,4,32,32]{0,3,2,1:T(8,128)(2,1)} %fusion) | data formatting | bytes 1048576 | tf_op jit(solution)/shard_map/convert_element_type | solution.py:76
  33.5 2.2 %reshape.58 = bf16[256,1024]{1,0:T(8,128)(2,1)S(1)} reshape(bf16[64,4,32,32]{3,2,1,0:T(8,128)(2,1)S(1)} %copy.35) | data formatting | bytes 1048576 | tf_op jit(solution)/shard_map/reshape | solution.py:76
  35.7 0.9 %convert_multiply_fusion = f32[64,4,128]{2,1,0:T(4,128)S(1)} fusion(bf16[64,4,128]{2,1,0:T(4,128)(2,1)} %param.11), kind=kLoop, calls=%fused_computation.18 | loop fusion | flops 65536 | bytes 196608 | tf_op jit(solution)/shard_map/mul | solution.py:84
  36.6 0.3 fusion.6
  36.9 0.7 all_to_all.12
  37.6 4.2 %all-to-all-start = ((bf16[16,4,512]{2,1,0:T(4,128)(2,1)}), bf16[16,4,512]{2,1,0:T(4,128)(2,1)}, u32[]{:S(2)}, u32[]{:S(2)}) async-start(bf16[16,4,512]{2,1,0:T(4,128)(2,1)} %all_to_all.12), calls=%async_computation | async-start | bytes 131072 | tf_op jit(solution)/shard_map/all_to_all | solution.py:96
  41.7 0.7 reshape.54
  42.5 0.3 fusion.2
  42.8 1.6 %reshape.61 = bf16[64,4,32,32]{3,2,1,0:T(8,128)(2,1)S(1)} reshape(bf16[256,1024]{1,0:T(8,128)(2,1)S(1)} %fusion.2) | data formatting | bytes 1048576 | tf_op jit(solution)/shard_map/reshape | solution.py:42
  44.4 1.3 %fusion.11 = (bf16[96,4,32]{0,2,1:T(8,128)(2,1)S(1)}, f32[96,4,32]{0,2,1:T(8,128)}) fusion(bf16[96,64,32,1]{0,2,3,1:T(8,128)(2,1)S(1)} %bitcast.49, bf16[64,4,32,32]{3,2,1,0:T(8,128)(2,1)S(1)} %reshape.61), kind=kOutput, calls=%fused_computation.21 | convolution fusion | flops 50343936 | bytes 991232 | tf_op jit(solution)/shard_map/ijcd,sic->sjd/dot_general | solution.py:92
  45.7 22.7 %all_gather.6 = bf16[96,2048]{1,0:T(8,128)(2,1)S(1)} all-gather(bf16[96,128]{1,0:T(8,128)(2,1)S(1)} %copy-done.1), channel_id=1, replica_groups=mesh['group'=2,'col'=16] {'col'}, dimensions={1}, use_global_device_ids=true | all-gather | bytes 417792 | tf_op jit(solution)/shard_map/all_gather | solution.py:52
  68.4 0.3 copy.29
  68.7 0.1 copy.41
  68.8 0.9 %copy.36 = bf16[4,16,512]{2,1,0:T(8,128)(2,1)S(1)} copy(bf16[4,16,512]{2,0,1:T(4,128)(2,1)} %bitcast.8) | data formatting | bytes 131072 | tf_op jit(solution)/shard_map/all_to_all | solution.py:96
  69.7 0.1 reshape.59
  69.7 0.3 fusion.1
  70.0 1.6 %reshape.71 = bf16[4,64,32,32]{3,2,1,0:T(8,128)(2,1)S(1)} reshape(bf16[256,1024]{1,0:T(8,128)(2,1)S(1)} %fusion.1) | data formatting | bytes 1048576 | tf_op jit(solution)/shard_map/reshape | solution.py:42
  71.6 1.3 %fusion.10 = (bf16[96,4,32]{0,2,1:T(8,128)(2,1)S(1)}, f32[96,4,32]{0,2,1:T(8,128)}) fusion(bf16[96,64,32,1]{0,2,1,3:T(8,128)(2,1)S(1)} %bitcast.50, bf16[4,64,32,32]{3,2,1,0:T(8,128)(2,1)S(1)} %reshape.71), kind=kOutput, calls=%fused_computation.20 | convolution fusion | flops 50343936 | bytes 991232 | tf_op jit(solution)/shard_map/ijcd,sjd->sic/dot_general | solution.py:110
  73.0 0.1 copy.40
  73.1 0.2 fusion.12
  73.3 0.2 fusion.3
  73.5 0.7 reshape.64
  (10 shorter events, 0.0 us)
Async XLA Ops:
  0.6 36.0 %copy-start = (bf16[1024,128]{1,0:T(8,128)(2,1)S(1)}, bf16[1024,128]{1,0:T(8,128)(2,1)}, u32[]{:S(2)}) copy-start(bf16[1024,128]{1,0:T(8,128)(2,1)} %param.9) | copy-start | bytes 786436
  0.6 26.7 %copy-start.3 = (bf16[256,32]{0,1:T(8,128)(2,1)S(1)}, bf16[256,32]{0,1:T(8,128)(2,1)}, u32[]{:S(2)}) copy-start(bf16[256,32]{0,1:T(8,128)(2,1)} %param.8) | copy-start | bytes 49156
  33.5 3.1 %copy-start.4 = (f32[128]{0:T(128)S(1)}, f32[128]{0:T(128)}, u32[]{:S(2)}) copy-start(f32[128]{0:T(128)} %param.10) | copy-start | bytes 1540
  37.6 31.2 %all-to-all-start = ((bf16[16,4,512]{2,1,0:T(4,128)(2,1)}), bf16[16,4,512]{2,1,0:T(4,128)(2,1)}, u32[]{:S(2)}, u32[]{:S(2)}) async-start(bf16[16,4,512]{2,1,0:T(4,128)(2,1)} %all_to_all.12), calls=%async_computation | async-start | bytes 131072 | tf_op jit(solution)/shard_map/all_to_all | solution.py:96
  42.8 3.0 %copy-start.1 = (bf16[96,128]{1,0:T(8,128)(2,1)S(1)}, bf16[96,128]{1,0:T(8,128)(2,1)}, u32[]{:S(2)}) copy-start(bf16[96,128]{1,0:T(8,128)(2,1)} %reshape.54) | copy-start | bytes 73732
  70.0 3.1 %copy-start.2 = (bf16[256,32]{0,1:T(8,128)(2,1)S(1)}, bf16[256,32]{0,1:T(8,128)(2,1)}, u32[]{:S(2)}) copy-start(bf16[256,32]{0,1:T(8,128)(2,1)} %param.7) | copy-start | bytes 49156
where the time goes:
time: 74.6 us; the launch traced here: 74.2 us
  blocking collectives  46.9 us (63%)
  local copies, waits for them, and re-layouts  14.9 us (20%)
  matrix products  6.57 us (9%)
  starting transfers between devices  4.16 us (6%)
  other arithmetic  0.87 us (1%)
  between operations  0.86 us (1%)
    all_gather x1, blocking collectives, per_device(): left_segment = lax.all_gather(first_operand_rows, 'col', axis=1, tiled=True)  24.2 us
    all_gather x1, blocking collectives, per_device(): lax.all_gather(second_operand_rows, 'col', axis=1, tiled=True)  22.7 us
    convert_element_type x1, local copies, waits for them, and re-layouts, per_device(): products.astype(jnp.bfloat16)  4.19 us
    all_to_all x1, starting transfers between devices, per_device(): lax.all_to_all(stored, 'col', split_axis=0, concat_axis=1, tiled=True)  4.16 us
    reshape x2, local copies, waits for them, and re-layouts, outer_slopes(): backward.astype(jnp.bfloat16)  3.16 us
    reshape x1, local copies, waits for them, and re-layouts, per_device(): products.astype(jnp.bfloat16)  2.23 us
    dot_general x1, matrix products, per_device(): jnp.einsum('sic,sjd->ijcd', left_block, second_operand_local, preferred_e...  1.63 us
    all_to_all x2, local copies, waits for them, and re-layouts, per_device(): lax.all_to_all(stored, 'col', split_axis=0, concat_axis=1, tiled=True)  1.52 us
  transfers between devices with their start and end apart: 1, of which 0 were waited for; matrix products, arithmetic and copies ran while one was open for 6% of the time, Pallas kernels for 0%

commit v1 on v0

--- a/solution.py
+++ b/solution.py
@@ -93,7 +93,10 @@
             "ijcd,sic->sjd", accumulate_slopes, left_block, preferred_element_type=jnp.float32
         )
     second_operand_gradient, stored, right_whole = (second_operand_gradient, stored, right_whole)
-    received = lax.all_to_all(stored, "col", split_axis=0, concat_axis=1, tiled=True)
+    size = lax.axis_size("col")
+    tiles = jnp.stack(jnp.split(stored, size, axis=0), axis=0)
+    tiles = lax.all_to_all(tiles, "col", split_axis=0, concat_axis=0)
+    received = jnp.concatenate(tiles, axis=1)
     right_all = right_whole.reshape(alignment_row_count, residue_total_count, operand_channel_width)
     col_span = local_residue_start * max(
         max(1, 96 // local_residue_start), lax.axis_size("col") // 8

time: 74.6 us -> 83.7 us (1.12)
  local copies, waits for them, and re-layouts: 14.9 us -> 23.9 us
    unnamed x10 -> x25, local copies, waits for them, and re-layouts: 0.03 us -> 8.98 us
    all_to_all x2 -> x0, local copies, waits for them, and re-layouts: 1.52 us -> none  [per_device(): lax.all_to_all(stored, 'col', split_axis=0, concat_axis=1, tiled=True)]
  transfers between devices with their start and end apart: 1 -> 1, of which waited for: 0 -> 0; matrix products, arithmetic and copies ran while one was open for 6% -> 5% of each run, Pallas kernels for 0% -> 0%
where the time goes in v1:
time: 83.7 us; the launch traced here: 83.3 us
  blocking collectives  46.9 us (56%)
  local copies, waits for them, and re-layouts  23.9 us (29%)
  matrix products  6.59 us (8%)
  starting transfers between devices  4.15 us (5%)
  between operations  0.89 us (1%)
  other arithmetic  0.87 us (1%)
    all_gather x1, blocking collectives, per_device(): left_segment = lax.all_gather(first_operand_rows, 'col', axis=1, tiled=True)  24.2 us
    all_gather x1, blocking collectives, per_device(): lax.all_gather(second_operand_rows, 'col', axis=1, tiled=True)  22.7 us
    unnamed x25, local copies, waits for them, and re-layouts  8.98 us
    convert_element_type x1, local copies, waits for them, and re-layouts, per_device(): products.astype(jnp.bfloat16)  4.19 us
    all_to_all x1, starting transfers between devices, per_device(): tiles = lax.all_to_all(tiles, 'col', split_axis=0, concat_axis=0)  4.15 us
    reshape x2, local copies, waits for them, and re-layouts, outer_slopes(): backward.astype(jnp.bfloat16)  3.16 us
    reshape x1, local copies, waits for them, and re-layouts, per_device(): products.astype(jnp.bfloat16)  2.23 us
  transfers between devices with their start and end apart: 1, of which 0 were waited for; matrix products, arithmetic and copies ran while one was open for 5% of the time, Pallas kernels for 0%

profile of v1, /device:TPU:0, one launch (start us, length us, event | category | flops | bytes accessed | tf_op | source)
XLA Modules:
  0.0 83.3 jit_solution(5390616384504252940)
XLA Ops:
  0.7 1.0 %reshape.80 = bf16[384,256]{1,0:T(8,128)(2,1)S(1)} reshape(bf16[96,4,256]{2,1,0:T(4,128)(2,1)} %param.6) | data formatting | bytes 393216 | tf_op jit(solution)/shard_map/reshape | solution.py:21
  1.7 0.9 %convolution_convert_fusion = bf16[384,32]{0,1:T(8,128)(2,1)S(1)} fusion(bf16[384,256]{1,0:T(8,128)(2,1)S(1)} %reshape.80, bf16[256,32]{0,1:T(8,128)(2,1)} %param.7), kind=kOutput, calls=%fused_computation.14 | convolution fusion | flops 6303744 | bytes 237568 | tf_op jit(solution)/shard_map/dot_general | solution.py:25
  2.8 24.2 %all_gather.7 = bf16[96,2048]{1,0:T(8,128)(2,1)S(1)} all-gather(bf16[96,128]{1,0:T(8,128)(2,1)S(1)} %reshape.83), channel_id=1, replica_groups=mesh['group'=2,'col'=16] {'col'}, dimensions={1}, use_global_device_ids=true | all-gather | bytes 417792 | tf_op jit(solution)/shard_map/all_gather | solution.py:51
  27.6 1.6 %fusion = bf16[64,4,32,32]{0,3,2,1:T(8,128)(2,1)} fusion(bf16[96,64,32]{0,2,1:T(8,128)(2,1)S(1)} %bitcast.48, bf16[96,4,32,1]{2,1,0,3:T(4,128)(2,1)S(1)} %bitcast.51), kind=kOutput, calls=%fused_computation.1 | convolution fusion | flops 50855936 | bytes 942080 | tf_op jit(solution)/shard_map/sic,sjd->ijcd/dot_general | solution.py:68
  29.3 4.2 %copy.50 = bf16[64,4,32,32]{3,2,1,0:T(8,128)(2,1)S(1)} copy(bf16[64,4,32,32]{0,3,2,1:T(8,128)(2,1)} %fusion) | data formatting | bytes 1048576 | tf_op jit(solution)/shard_map/convert_element_type | solution.py:76
  33.5 2.2 %reshape.85 = bf16[256,1024]{1,0:T(8,128)(2,1)S(1)} reshape(bf16[64,4,32,32]{3,2,1,0:T(8,128)(2,1)S(1)} %copy.50) | data formatting | bytes 1048576 | tf_op jit(solution)/shard_map/reshape | solution.py:76
  35.7 0.9 %convert_multiply_fusion = f32[64,4,128]{2,1,0:T(4,128)S(1)} fusion(bf16[64,4,128]{2,1,0:T(4,128)(2,1)} %param.11), kind=kLoop, calls=%fused_computation.18 | loop fusion | flops 65536 | bytes 196608 | tf_op jit(solution)/shard_map/mul | solution.py:84
  36.9 0.6 constant_dynamic-update-slice_fusion.15
  37.7 0.6 constant_dynamic-update-slice_fusion.14
  38.3 0.6 constant_dynamic-update-slice_fusion.13
  38.9 0.6 constant_dynamic-update-slice_fusion.12
  39.5 0.6 constant_dynamic-update-slice_fusion.11
  40.1 0.6 constant_dynamic-update-slice_fusion.10
  40.7 0.6 constant_dynamic-update-slice_fusion.9
  41.3 0.6 constant_dynamic-update-slice_fusion.8
  41.9 0.6 constant_dynamic-update-slice_fusion.7
  42.5 0.6 constant_dynamic-update-slice_fusion.6
  43.1 0.6 constant_dynamic-update-slice_fusion.5
  43.7 0.6 constant_dynamic-update-slice_fusion.4
  44.3 0.6 constant_dynamic-update-slice_fusion.3
  44.9 0.6 constant_dynamic-update-slice_fusion.2
  45.5 0.6 constant_dynamic-update-slice_fusion.1
  46.1 0.6 constant_dynamic-update-slice_fusion
  46.7 4.2 %all-to-all-start = ((bf16[16,4,512]{2,1,0:T(4,128)(2,1)}), bf16[16,4,512]{2,1,0:T(4,128)(2,1)}, u32[]{:S(2)}, u32[]{:S(2)}) async-start(bf16[16,4,512]{2,1,0:T(4,128)(2,1)} %constant_dynamic-update-slice_fusion), calls=%async_computation | async-start | bytes 131072 | tf_op jit(solution)/shard_map/all_to_all | solution.py:98
  50.8 0.7 reshape.81
  51.9 1.6 %reshape.88 = bf16[64,4,32,32]{3,2,1,0:T(8,128)(2,1)S(1)} reshape(bf16[256,1024]{1,0:T(8,128)(2,1)S(1)} %fusion.2) | data formatting | bytes 1048576 | tf_op jit(solution)/shard_map/reshape | solution.py:42
  53.4 1.3 %fusion.12 = (bf16[96,4,32]{0,2,1:T(8,128)(2,1)S(1)}, f32[96,4,32]{0,2,1:T(8,128)}) fusion(bf16[96,64,32,1]{0,2,3,1:T(8,128)(2,1)S(1)} %bitcast.49, bf16[64,4,32,32]{3,2,1,0:T(8,128)(2,1)S(1)} %reshape.88), kind=kOutput, calls=%fused_computation.38 | convolution fusion | flops 50343936 | bytes 991232 | tf_op jit(solution)/shard_map/ijcd,sic->sjd/dot_general | solution.py:92
  54.8 22.7 %all_gather.6 = bf16[96,2048]{1,0:T(8,128)(2,1)S(1)} all-gather(bf16[96,128]{1,0:T(8,128)(2,1)S(1)} %copy-done.1), channel_id=1, replica_groups=mesh['group'=2,'col'=16] {'col'}, dimensions={1}, use_global_device_ids=true | all-gather | bytes 417792 | tf_op jit(solution)/shard_map/all_gather | solution.py:52
  77.9 0.9 %copy.51 = bf16[4,16,512]{2,1,0:T(8,128)(2,1)S(1)} copy(bf16[4,16,512]{2,0,1:T(4,128)(2,1)} %bitcast.8) | data formatting | bytes 131072 | tf_op jit(solution)/shard_map/reshape | solution.py:99
  79.1 1.6 %reshape.98 = bf16[4,64,32,32]{3,2,1,0:T(8,128)(2,1)S(1)} reshape(bf16[256,1024]{1,0:T(8,128)(2,1)S(1)} %fusion.1) | data formatting | bytes 1048576 | tf_op jit(solution)/shard_map/reshape | solution.py:42
  80.7 1.3 %fusion.11 = (bf16[96,4,32]{0,2,1:T(8,128)(2,1)S(1)}, f32[96,4,32]{0,2,1:T(8,128)}) fusion(bf16[96,64,32,1]{0,2,1,3:T(8,128)(2,1)S(1)} %bitcast.50, bf16[4,64,32,32]{3,2,1,0:T(8,128)(2,1)S(1)} %reshape.98), kind=kOutput, calls=%fused_computation.37 | convolution fusion | flops 50343936 | bytes 991232 | tf_op jit(solution)/shard_map/ijcd,sjd->sic/dot_general | solution.py:113
  82.6 0.7 reshape.91
  (42 shorter events, 2.9 us)
Async XLA Ops:
  0.6 36.0 %copy-start = (bf16[1024,128]{1,0:T(8,128)(2,1)S(1)}, bf16[1024,128]{1,0:T(8,128)(2,1)}, u32[]{:S(2)}) copy-start(bf16[1024,128]{1,0:T(8,128)(2,1)} %param.9) | copy-start | bytes 786436
  0.6 26.7 %copy-start.3 = (bf16[256,32]{0,1:T(8,128)(2,1)S(1)}, bf16[256,32]{0,1:T(8,128)(2,1)}, u32[]{:S(2)}) copy-start(bf16[256,32]{0,1:T(8,128)(2,1)} %param.8) | copy-start | bytes 49156
  33.5 3.1 %copy-start.4 = (f32[128]{0:T(128)S(1)}, f32[128]{0:T(128)}, u32[]{:S(2)}) copy-start(f32[128]{0:T(128)} %param.10) | copy-start | bytes 1540
  46.7 31.2 %all-to-all-start = ((bf16[16,4,512]{2,1,0:T(4,128)(2,1)}), bf16[16,4,512]{2,1,0:T(4,128)(2,1)}, u32[]{:S(2)}, u32[]{:S(2)}) async-start(bf16[16,4,512]{2,1,0:T(4,128)(2,1)} %constant_dynamic-update-slice_fusion), calls=%async_computation | async-start | bytes 131072 | tf_op jit(solution)/shard_map/all_to_all | solution.py:98
  51.8 3.0 %copy-start.1 = (bf16[96,128]{1,0:T(8,128)(2,1)S(1)}, bf16[96,128]{1,0:T(8,128)(2,1)}, u32[]{:S(2)}) copy-start(bf16[96,128]{1,0:T(8,128)(2,1)} %reshape.81) | copy-start | bytes 73732
  79.1 3.1 %copy-start.2 = (bf16[256,32]{0,1:T(8,128)(2,1)S(1)}, bf16[256,32]{0,1:T(8,128)(2,1)}, u32[]{:S(2)}) copy-start(bf16[256,32]{0,1:T(8,128)(2,1)} %param.7) | copy-start | bytes 49156
